TPU v7x, 32 devices: a whole 2x2x4 slice. The times are simulated.
32 devices in a mesh: groups: 2 (over x), chan: 16 (over z, y, core).
Axes of the slice: x: 2, y: 2, z: 4, core: 2. Of those that a mesh axis runs over, the one named last changes fastest.
Arguments:
- waveforms: bfloat16 [10240, 15360], P('chan', 'groups'), parts along dimension 1, may hold values from -250 to 250
- basis: bfloat16 [16, 10240, 200], P(None, 'chan'), may hold values from -1 to 1
- bounds: int32 [2, 768], replicated, may hold values from 0 to 5120, as said below
Outputs:
- detection: float32 [15360], P(('groups', 'chan')), parts along dimension 0
- coefficients: float32 [16, 15360], P(None, ('groups', 'chan')), parts along dimension 1
There are 2 independent parts, one for each index of `groups`. A program takes and returns all parts, laid end to end along the dimension named above; an argument that names none is the same for every part. Nothing has to cross between parts.
Inputs may be any that keep to these rules, and one draw needn't show every extreme that they name: bounds[0, 0] is 0 and every bounds[0, f] is below 160; bounds[1, f] grows roughly in proportion to f and is 5120 at the last bin; where bounds[0, f] exceeds bounds[1, f] nothing passes.
All inputs are finite; a program needn't handle non-finite values.
Results may differ from a plain program's by a relative error of at most 0.017.
Values may be sent and summed in bfloat16 or wider, within the bound.
A program may use at most 128 MiB of HBM per device.

v0:
```python
import math
import jax
import jax.numpy as jnp
from jax import lax
from jax.sharding import PartitionSpec as P

time_blocks = 4
basis_blocks = 4
highest = lax.Precision.HIGHEST


def angle_lookup(row_ids, col_ids, modulus):
    rotation_radians = (row_ids[:, None] * col_ids[None, :] % modulus).astype(jnp.float32) * (
        2.0 * math.pi / modulus
    )
    return (jnp.cos(rotation_radians), jnp.sin(rotation_radians))


def rotate(layout, cos_table, sin_table, real_part, imag_part, orientation):
    cos_real = jnp.einsum(layout, cos_table, real_part, precision=highest)
    cos_imag = jnp.einsum(layout, cos_table, imag_part, precision=highest)
    sin_real = jnp.einsum(layout, sin_table, real_part, precision=highest)
    sin_imag = jnp.einsum(layout, sin_table, imag_part, precision=highest)
    return (cos_real - orientation * sin_imag, cos_imag + orientation * sin_real)


def apply_twist(cos_table, sin_table, real_part, imag_part, orientation):
    return (
        cos_table * real_part - orientation * sin_table * imag_part,
        cos_table * imag_part + orientation * sin_table * real_part,
    )


def count_ids(count):
    return jnp.arange(count, dtype=jnp.int32)


def block_table(base_tables, freq_ids, offset, recorded_readings):
    base_cos, base_sin = base_tables
    shift_cos, shift_sin = angle_lookup(freq_ids, jnp.reshape(offset, (1,)), recorded_readings)
    cos_table = base_cos * shift_cos - base_sin * shift_sin
    sin_table = base_sin * shift_cos + base_cos * shift_sin
    return jnp.stack([cos_table, -sin_table]).astype(jnp.bfloat16)


def temporal_spectrum(waveforms, base_tables, layout, output_dims):
    recorded_readings = waveforms.shape[1]
    block_width = recorded_readings // time_blocks
    freq_ids = count_ids(base_tables[0].shape[0])

    def temporal_advance(running, block_id):
        offset = block_id * block_width
        dft_table = block_table(base_tables, freq_ids, offset, recorded_readings)
        segment = lax.dynamic_slice_in_dim(waveforms, offset, block_width, 1)
        return (
            running + jnp.einsum(layout, dft_table, segment, preferred_element_type=jnp.float32),
            None,
        )

    spectrum, _ = lax.scan(
        temporal_advance, jnp.zeros(output_dims, jnp.float32), count_ids(time_blocks)
    )
    return spectrum.astype(jnp.bfloat16)


def frequency_filter(local_spectrum, band_edges):
    values = local_spectrum.astype(jnp.float32)
    bin_count, full_count = (values.shape[1], values.shape[2])
    devices = lax.axis_size("chan")
    block_width = full_count // devices
    real_part = values[0].reshape(bin_count, devices, block_width)
    imag_part = values[1].reshape(bin_count, devices, block_width)
    cos_parts, sine_components = angle_lookup(count_ids(devices), count_ids(devices), devices)
    cos_width, sin_width = angle_lookup(count_ids(block_width), count_ids(block_width), block_width)
    cos_twist, sin_twist = angle_lookup(count_ids(devices), count_ids(block_width), full_count)
    real_part, imag_part = rotate(
        "kp,fpm->fkm", cos_parts, sine_components, real_part, imag_part, -1.0
    )
    real_part, imag_part = apply_twist(cos_twist, sin_twist, real_part, imag_part, -1.0)
    real_part, imag_part = rotate("mn,fkm->fkn", cos_width, sin_width, real_part, imag_part, -1.0)
    wave_ids = count_ids(devices)[:, None] + devices * count_ids(block_width)[None, :]
    magnitude = jnp.where(wave_ids > full_count // 2, full_count - wave_ids, wave_ids)[None]
    passing = (magnitude >= band_edges[0][:, None, None]) & (
        magnitude <= band_edges[1][:, None, None]
    )
    real_part = jnp.where(passing, real_part, 0.0)
    imag_part = jnp.where(passing, imag_part, 0.0)
    real_part, imag_part = rotate("mn,fkn->fkm", cos_width, sin_width, real_part, imag_part, 1.0)
    real_part, imag_part = apply_twist(cos_twist, sin_twist, real_part, imag_part, 1.0)
    real_part, imag_part = rotate(
        "kp,fkm->fpm", cos_parts, sine_components, real_part, imag_part, 1.0
    )
    restored = jnp.stack([real_part, imag_part]).reshape(2, bin_count, full_count) * (
        1.0 / full_count
    )
    return restored.astype(jnp.bfloat16)


def coefficient_spectra(basis, filtered, layout, frequencies, recorded_readings):
    basis_rank, channels, tap_count = basis.shape
    cos_table, sin_table = angle_lookup(
        count_ids(frequencies), count_ids(tap_count), recorded_readings
    )
    dft_table = jnp.stack([cos_table, -sin_table]).astype(jnp.bfloat16)
    filtered_real = filtered[0].astype(jnp.float32)
    filtered_imag = filtered[1].astype(jnp.float32)
    contract = "kfm," + layout + "->kf"
    basis_group = basis.reshape(basis_blocks, basis_rank // basis_blocks, channels, tap_count)

    def project(members):
        transformed = jnp.einsum(
            "kml,rfl->krfm", members, dft_table, preferred_element_type=jnp.float32
        )
        trans_real, trans_imag = (transformed[:, 0], transformed[:, 1])
        spectra_real = jnp.einsum(
            contract, trans_real, filtered_real, precision=highest
        ) + jnp.einsum(contract, trans_imag, filtered_imag, precision=highest)
        fourier_quadrature = jnp.einsum(
            contract, trans_real, filtered_imag, precision=highest
        ) - jnp.einsum(contract, trans_imag, filtered_real, precision=highest)
        return jnp.stack([spectra_real, fourier_quadrature], axis=1)

    return lax.map(project, basis_group).reshape(basis_rank, 2, frequencies)


def channel_power(filtered, base_tables, layout, frequencies, recorded_readings):
    freq_ids = count_ids(frequencies)
    weights = jnp.where(freq_ids == 0, 1.0, 2.0).astype(jnp.bfloat16)
    weighted = filtered * weights[None, :, None]
    block_width = recorded_readings // time_blocks
    contract = "r" + layout + ",rft->mt"

    def channel_advance(running, block_id):
        offset = block_id * block_width
        dft_table = block_table(base_tables, freq_ids, offset, recorded_readings)
        traces = jnp.einsum(contract, weighted, dft_table, preferred_element_type=jnp.float32) * (
            1.0 / recorded_readings
        )
        return (running, jnp.sum(traces * traces, axis=0))

    _, pieces = lax.scan(channel_advance, jnp.zeros((), jnp.float32), count_ids(time_blocks))
    return pieces.reshape(recorded_readings)


def local(waveforms, basis, bounds):
    devices = lax.axis_size("chan")
    position = lax.axis_index("chan")
    channels, recorded_readings = waveforms.shape
    basis_rank, _, tap_count = basis.shape
    frequencies = bounds.shape[1]
    full_count = channels * devices
    freq_ids = count_ids(frequencies)
    base_tables = angle_lookup(
        freq_ids, count_ids(recorded_readings // time_blocks), recorded_readings
    )
    layout = "fm"
    spectrum = temporal_spectrum(waveforms, base_tables, "rft,mt->rfm", (2, frequencies, channels))
    local_spectrum = lax.all_to_all(spectrum, "chan", split_axis=1, concat_axis=2, tiled=True)
    bin_count = local_spectrum.shape[1]
    band_edges = lax.dynamic_slice_in_dim(bounds, position * bin_count, bin_count, 1)
    filtered = lax.all_to_all(
        frequency_filter(local_spectrum, band_edges),
        "chan",
        split_axis=2,
        concat_axis=1,
        tiled=True,
    )
    spectra = coefficient_spectra(basis, filtered, layout, frequencies, recorded_readings)
    flattened = basis.reshape(basis_rank, channels * tap_count)
    gram_matrix = jnp.einsum("ka,ja->kj", flattened, flattened, preferred_element_type=jnp.float32)
    trace_power = channel_power(filtered, base_tables, layout, frequencies, recorded_readings)
    spectra, gram_matrix, trace_power = lax.psum((spectra, gram_matrix, trace_power), "chan")
    lag_count = recorded_readings // devices
    lag_start = position * lag_count
    cos_lags, sin_lags = angle_lookup(freq_ids, lag_start + count_ids(lag_count), recorded_readings)
    weights = jnp.where(freq_ids == 0, 1.0, 2.0).astype(jnp.float32)
    scaled_inphase = spectra[:, 0] * weights[None, :]
    weighted_imag = spectra[:, 1] * weights[None, :]
    correlation = (
        jnp.dot(scaled_inphase, cos_lags, precision=highest)
        - jnp.dot(weighted_imag, sin_lags, precision=highest)
    ) * (1.0 / recorded_readings)
    extended = jnp.concatenate([trace_power, trace_power[:tap_count]])
    running = jnp.concatenate([jnp.zeros((1,), jnp.float32), jnp.cumsum(extended)])
    energy = lax.dynamic_slice_in_dim(
        running, lag_start + tap_count, lag_count, 0
    ) - lax.dynamic_slice_in_dim(running, lag_start, lag_count, 0)
    energy_threshold = energy / (full_count * tap_count) + 1e-06
    cholesky_factor = jnp.linalg.cholesky(gram_matrix)
    solved = jax.scipy.linalg.cho_solve((cholesky_factor, True), correlation)
    detection = jnp.sum(correlation * solved, axis=0) / (basis_rank * energy_threshold)
    coefficients = correlation / jnp.sqrt(energy_threshold)[None, :]
    return (detection, coefficients)


def solution(mesh):
    in_specs = (P("chan", "groups"), P(None, "chan", None), P())
    out_specs = (P(("groups", "chan")), P(None, ("groups", "chan")))
    return jax.shard_map(local, mesh=mesh, in_specs=in_specs, out_specs=out_specs, check_vma=False)
```

profile of v0, /device:TPU:0, one launch (start us, length us, event | category | flops | bytes accessed | tf_op | source)
XLA Modules:
  0.0 827.4 jit_solution(9234787007890897605)
XLA Ops:
  7.2 148.7 %while.40 = (s32[]{:T(128)}, f32[2,768,640]{2,1,0:T(8,128)}, s32[4]{0:T(128)S(1)}, bf16[640,7680]{1,0:T(8,128)(2,1)}, s32[]{:T(128)}, /*index=5*/s32[]{:T(128)}, s32[1]{0:T(128)}, s32[]{:T(128)}) while((s32[]{:T(128)}, f32[2,768,640]{2,1,0:T(8,128)}, s32[4]{0:T(128)S(1)}, bf16[640,7680]{1,0:T(8,128)(2,1)}, s32[]{:T(128)}, ...), condition=%wide.region_1.2_spmd.clone.clone, body=%wide.region_0.1_spmd.clone.clone.sunk | while | flops 3806337792 | bytes 53588192 | solution.py:60
  8.5 25.9 %fusion.331 = (bf16[1,768,1920]{2,1,0:T(8,128)(2,1)S(1)}, bf16[1,768,1920]{2,1,0:T(8,128)(2,1)S(1)}) fusion(f32[768]{0:T(1024)S(1)} %get-tuple-element.499, f32[768]{0:T(1024)S(1)} %get-tuple-element.500), kind=kLoop, calls=%fused_computation.52.clone.1 | loop fusion | flops 26542080 | bytes 5904384 | tf_op jit(solution)/shard_map/convert
  45.7 25.9 %fusion.331 = (bf16[1,768,1920]{2,1,0:T(8,128)(2,1)S(1)}, bf16[1,768,1920]{2,1,0:T(8,128)(2,1)S(1)}) fusion(f32[768]{0:T(1024)S(1)} %get-tuple-element.499, f32[768]{0:T(1024)S(1)} %get-tuple-element.500), kind=kLoop, calls=%fused_computation.52.clone.1 | loop fusion | flops 26542080 | bytes 5904384 | tf_op jit(solution)/shard_map/convert
  82.9 25.9 %fusion.331 = (bf16[1,768,1920]{2,1,0:T(8,128)(2,1)S(1)}, bf16[1,768,1920]{2,1,0:T(8,128)(2,1)S(1)}) fusion(f32[768]{0:T(1024)S(1)} %get-tuple-element.499, f32[768]{0:T(1024)S(1)} %get-tuple-element.500), kind=kLoop, calls=%fused_computation.52.clone.1 | loop fusion | flops 26542080 | bytes 5904384 | tf_op jit(solution)/shard_map/convert
  120.1 25.9 %fusion.331 = (bf16[1,768,1920]{2,1,0:T(8,128)(2,1)S(1)}, bf16[1,768,1920]{2,1,0:T(8,128)(2,1)S(1)}) fusion(f32[768]{0:T(1024)S(1)} %get-tuple-element.499, f32[768]{0:T(1024)S(1)} %get-tuple-element.500), kind=kLoop, calls=%fused_computation.52.clone.1 | loop fusion | flops 26542080 | bytes 5904384 | tf_op jit(solution)/shard_map/convert
  170.5 38.0 %all-to-all-done = bf16[2,768,640]{2,0,1:T(2,128)(2,1)S(1)} async-done(((bf16[2,768,640]{2,0,1:T(2,128)(2,1)}), bf16[2,768,640]{2,0,1:T(2,128)(2,1)S(1)}, u32[]{:S(2)}, u32[]{:S(2)}) %all-to-all-start) | async-done | bytes 1966112 | tf_op jit(solution)/shard_map/all_to_all | solution.py:158
  213.6 11.9 %fusion.89 = f32[48,16,640]{2,1,0:T(8,128)S(1)} fusion(f32[48,640,16]{1,2,0:T(8,128)S(1)} %multiply_add_fusion.1, f32[48,640,16]{1,2,0:T(8,128)S(1)} %multiply_subtract_fusion.1, f32[16,640]{1,0:T(8,128)S(1)} %get-tuple-element.385, f32[16,640]{1,0:T(8,128)S(1)} %get-tuple-element.384), kind=kOutput, calls=%fused_computation.124 | convolution fusion | flops 3780034560 | bytes 5980160 | tf_op jit(solution)/shard_map/mn,fkm->fkn/dot_general | solution.py:22
  225.5 11.7 %fusion.91 = f32[48,16,640]{2,1,0:T(8,128)S(1)} fusion(f32[48,640,16]{1,2,0:T(8,128)S(1)} %multiply_add_fusion.1, f32[48,640,16]{1,2,0:T(8,128)S(1)} %multiply_subtract_fusion.1, f32[16,640]{1,0:T(8,128)S(1)} %get-tuple-element.385, f32[16,640]{1,0:T(8,128)S(1)} %get-tuple-element.384), kind=kOutput, calls=%fused_computation.126 | convolution fusion | flops 3780034560 | bytes 5980160 | tf_op jit(solution)/shard_map/mn,fkm->fkn/dot_general | solution.py:23
  237.3 11.8 %add_select_fusion.6 = f32[48,16,640]{2,1,0:T(8,128)S(1)} fusion(f32[48,16,640]{2,1,0:T(8,128)S(1)} %fusion.89, s32[16,640]{1,0:T(8,128)S(1)} %compare_select_fusion, s32[48]{0:T(128)S(1)} %get-tuple-element.381, s32[48]{0:T(128)S(1)} %get-tuple-element.380, f32[48,640,16]{1,2,0:T(8,128)S(1)} %multiply_add_fusion.1, ...), kind=kOutput, calls=%fused_computation.113 | convolution fusion | flops 3782983680 | bytes 7987584 | tf_op jit(solution)/shard_map/mn,fkm->fkn/dot_general | solution.py:21
  249.0 11.8 %fusion.87 = f32[48,16,640]{2,1,0:T(8,128)S(1)} fusion(f32[48,16,640]{2,1,0:T(8,128)S(1)} %add_select_fusion.6), kind=kOutput, calls=%fused_computation.122 | convolution fusion | flops 3778560000 | bytes 3932160 | tf_op jit(solution)/shard_map/mn,fkn->fkm/dot_general | solution.py:23
  260.9 11.7 %subtract_select_fusion = f32[48,16,640]{2,1,0:T(8,128)S(1)} fusion(f32[48,16,640]{2,1,0:T(8,128)S(1)} %fusion.91, s32[16,640]{1,0:T(8,128)S(1)} %compare_select_fusion, s32[48]{0:T(128)S(1)} %get-tuple-element.381, s32[48]{0:T(128)S(1)} %get-tuple-element.380, f32[48,640,16]{1,2,0:T(8,128)S(1)} %multiply_add_fusion.1, ...), kind=kOutput, calls=%fused_computation.114 | convolution fusion | flops 3782983680 | bytes 7987584 | tf_op jit(solution)/shard_map/mn,fkm->fkn/dot_general | solution.py:20
  272.6 11.6 %fusion.85 = f32[48,16,640]{2,1,0:T(8,128)S(1)} fusion(f32[48,16,640]{2,1,0:T(8,128)S(1)} %subtract_select_fusion), kind=kOutput, calls=%fused_computation.120 | convolution fusion | flops 3778560000 | bytes 3932160 | tf_op jit(solution)/shard_map/mn,fkn->fkm/dot_general | solution.py:22
  284.2 11.9 %fusion.114 = f32[48,16,640]{2,1,0:T(8,128)S(1)} fusion(f32[48,16,640]{2,1,0:T(8,128)S(1)} %fusion.87, f32[48,16,640]{2,1,0:T(8,128)S(1)} %subtract_select_fusion), kind=kOutput, calls=%fused_computation.142 | convolution fusion | flops 3779051520 | bytes 5898240 | tf_op jit(solution)/shard_map/mn,fkn->fkm/dot_general | solution.py:20
  296.2 11.5 %fusion.117 = f32[48,16,640]{2,1,0:T(8,128)S(1)} fusion(f32[48,16,640]{2,1,0:T(8,128)S(1)} %fusion.85, f32[48,16,640]{2,1,0:T(8,128)S(1)} %add_select_fusion.6), kind=kOutput, calls=%fused_computation.143 | convolution fusion | flops 3779051520 | bytes 5898240 | tf_op jit(solution)/shard_map/mn,fkn->fkm/dot_general | solution.py:21
  331.0 11.3 %copy.99 = bf16[2,48,10240]{1,0,2:T(2,128)(2,1)} copy(bf16[2,48,10240]{2,1,0:T(8,128)(2,1)} %fusion.80) | data formatting | bytes 3932160 | tf_op jit(solution)/shard_map/convert_element_type | solution.py:96
  371.3 30.8 %all-to-all-done.1 = bf16[16,2,30720]{2,1,0:T(2,128)(2,1)S(1)} async-done(((bf16[16,2,30720]{2,1,0:T(2,128)(2,1)}), bf16[16,2,30720]{2,1,0:T(2,128)(2,1)S(1)}, u32[]{:S(2)}, u32[]{:S(2)}) %all-to-all-start.1) | async-done | bytes 1966112 | tf_op jit(solution)/shard_map/all_to_all | solution.py:161
  433.0 126.7 %while.39 = (s32[]{:T(128)}, f32[4,1920]{1,0:T(4,128)S(1)}, s32[4]{0:T(128)S(1)}, bf16[2,768,640]{1,2,0:T(8,128)(2,1)}, s32[]{:T(128)}, /*index=5*/s32[1]{0:T(128)}, s32[]{:T(128)}) while((s32[]{:T(128)}, f32[4,1920]{1,0:T(4,128)S(1)}, s32[4]{0:T(128)S(1)}, bf16[2,768,640]{1,2,0:T(8,128)(2,1)}, s32[]{:T(128)}, ...), condition=%wide.region_11.12_spmd.clone.clone, body=%wide.region_9.11_spmd.clone.clone.sunk | while | flops 3808056064 | bytes 21677712 | solution.py:141
  434.3 25.9 %fusion.326 = (bf16[1,768,1920]{2,1,0:T(8,128)(2,1)S(1)}, bf16[1,768,1920]{2,1,0:T(8,128)(2,1)S(1)}) fusion(f32[768]{0:T(1024)S(1)} %get-tuple-element.491, f32[768]{0:T(1024)S(1)} %get-tuple-element.492), kind=kLoop, calls=%fused_computation.16.clone.1 | loop fusion | flops 26542080 | bytes 5904384 | tf_op jit(solution)/shard_map/convert.2
  466.0 25.9 %fusion.326 = (bf16[1,768,1920]{2,1,0:T(8,128)(2,1)S(1)}, bf16[1,768,1920]{2,1,0:T(8,128)(2,1)S(1)}) fusion(f32[768]{0:T(1024)S(1)} %get-tuple-element.491, f32[768]{0:T(1024)S(1)} %get-tuple-element.492), kind=kLoop, calls=%fused_computation.16.clone.1 | loop fusion | flops 26542080 | bytes 5904384 | tf_op jit(solution)/shard_map/convert.2
  497.7 25.9 %fusion.326 = (bf16[1,768,1920]{2,1,0:T(8,128)(2,1)S(1)}, bf16[1,768,1920]{2,1,0:T(8,128)(2,1)S(1)}) fusion(f32[768]{0:T(1024)S(1)} %get-tuple-element.491, f32[768]{0:T(1024)S(1)} %get-tuple-element.492), kind=kLoop, calls=%fused_computation.16.clone.1 | loop fusion | flops 26542080 | bytes 5904384 | tf_op jit(solution)/shard_map/convert.2
  529.3 25.9 %fusion.326 = (bf16[1,768,1920]{2,1,0:T(8,128)(2,1)S(1)}, bf16[1,768,1920]{2,1,0:T(8,128)(2,1)S(1)}) fusion(f32[768]{0:T(1024)S(1)} %get-tuple-element.491, f32[768]{0:T(1024)S(1)} %get-tuple-element.492), kind=kLoop, calls=%fused_computation.16.clone.1 | loop fusion | flops 26542080 | bytes 5904384 | tf_op jit(solution)/shard_map/convert.2
  559.7 67.2 %all-reduce.1 = (f32[16,16]{0,1:T(8,128)S(1)}, f32[7680]{0:T(1024)S(1)}) all-reduce(f32[16,16]{0,1:T(8,128)S(1)} %fusion.142, f32[7680]{0:T(1024)S(1)} %reshape.545), channel_id=1, replica_groups=mesh['groups'=2,'chan'=16] {'chan'}, use_global_device_ids=true, to_apply=%region_5.6 | all-reduce | flops 7936 | bytes 63488 | tf_op jit(solution)/shard_map/psum | solution.py:172
  631.7 84.8 %while.38 = (s32[]{:T(128)}, f32[4,4,2,768]{3,2,1,0:T(2,128)S(1)}, bf16[4,4,640,200]{2,3,1,0:T(8,128)(2,1)}, bf16[2,768,200]{1,2,0:T(8,128)(2,1)S(1)}, f32[768,640]{1,0:T(8,128)}, /*index=5*/f32[768,640]{1,0:T(8,128)}, s32[]{:T(128)}) while((s32[]{:T(128)}, f32[4,4,2,768]{3,2,1,0:T(2,128)S(1)}, bf16[4,4,640,200]{2,3,1,0:T(8,128)(2,1)}, ...), condition=%wide.region_3.4_spmd, body=%wide.region_2.3_spmd.sunk | while | flops 1588592640 | bytes 45113436 | solution.py:123
  721.3 82.0 %all-reduce.4.cloned.1.call-done = f32[16,2,768]{2,1,0:T(2,128)} async-done(((f32[16,2,768]{2,1,0:T(2,128)}), f32[16,2,768]{2,1,0:T(2,128)}) %all-reduce.4.cloned.1.call-update) | async-done | bytes 98320 | tf_op jit(solution)/shard_map/psum | solution.py:172
  (165 shorter events, 276.1 us)
Async XLA Ops:
  7.2 162.8 %copy-start = (s32[2,768]{1,0:T(2,128)S(1)}, s32[2,768]{1,0:T(2,128)}, u32[]{:S(2)}) copy-start(s32[2,768]{1,0:T(2,128)} %param.11) | copy-start | bytes 18436
  8.5 25.9 %copy-start.5 = (f32[2,768,640]{2,1,0:T(8,128)S(1)}, f32[2,768,640]{2,1,0:T(8,128)}, u32[]{:S(2)}) copy-start(f32[2,768,640]{2,1,0:T(8,128)} %get-tuple-element.512) | copy-start | bytes 11796484 | tf_op jit(solution)/shard_map/while
  42.5 1.9 copy-start.6
  45.7 25.9 %copy-start.5 = (f32[2,768,640]{2,1,0:T(8,128)S(1)}, f32[2,768,640]{2,1,0:T(8,128)}, u32[]{:S(2)}) copy-start(f32[2,768,640]{2,1,0:T(8,128)} %get-tuple-element.512) | copy-start | bytes 11796484 | tf_op jit(solution)/shard_map/while
  79.7 1.9 copy-start.6
  82.9 25.9 %copy-start.5 = (f32[2,768,640]{2,1,0:T(8,128)S(1)}, f32[2,768,640]{2,1,0:T(8,128)}, u32[]{:S(2)}) copy-start(f32[2,768,640]{2,1,0:T(8,128)} %get-tuple-element.512) | copy-start | bytes 11796484 | tf_op jit(solution)/shard_map/while
  116.9 1.9 copy-start.6
  120.1 25.9 %copy-start.5 = (f32[2,768,640]{2,1,0:T(8,128)S(1)}, f32[2,768,640]{2,1,0:T(8,128)}, u32[]{:S(2)}) copy-start(f32[2,768,640]{2,1,0:T(8,128)} %get-tuple-element.512) | copy-start | bytes 11796484 | tf_op jit(solution)/shard_map/while
  154.1 1.9 copy-start.6
  162.4 46.1 %all-to-all-start = ((bf16[2,768,640]{2,0,1:T(2,128)(2,1)}), bf16[2,768,640]{2,0,1:T(2,128)(2,1)S(1)}, u32[]{:S(2)}, u32[]{:S(2)}) async-start(bf16[2,768,640]{2,0,1:T(2,128)(2,1)} %copy.169), calls=%async_computation | async-start | bytes 3932160 | tf_op jit(solution)/shard_map/all_to_all | solution.py:158
  307.7 5.4 copy-start.2
  324.7 2.9 copy-start.4
  352.7 49.4 %all-to-all-start.1 = ((bf16[16,2,30720]{2,1,0:T(2,128)(2,1)}), bf16[16,2,30720]{2,1,0:T(2,128)(2,1)S(1)}, u32[]{:S(2)}, u32[]{:S(2)}) async-start(bf16[16,2,30720]{2,1,0:T(2,128)(2,1)} %reshape.584), calls=%async_computation.1 | async-start | bytes 3932160 | tf_op jit(solution)/shard_map/all_to_all | solution.py:161
  363.4 439.9 %all-reduce.4.cloned.1.call-start = ((), (), s32[]{:S(2)}) async-start(), calls=%async_computation.2 | async-start | bytes 196608 | tf_op jit(solution)/shard_map/psum | solution.py:172
  433.0 194.6 %copy-start.3 = (bf16[2,48,16,640]{3,2,1,0:T(8,128)(2,1)S(1)}, bf16[2,48,16,640]{3,2,1,0:T(8,128)(2,1)}, u32[]{:S(2)}) copy-start(bf16[2,48,16,640]{3,2,1,0:T(8,128)(2,1)} %copy.146) | copy-start | bytes 5898244
  434.3 25.9 %copy-start.7 = (bf16[2,768,640]{1,2,0:T(8,128)(2,1)S(1)}, bf16[2,768,640]{1,2,0:T(8,128)(2,1)}, u32[]{:S(2)}) copy-start(bf16[2,768,640]{1,2,0:T(8,128)(2,1)} %get-tuple-element.544) | copy-start | bytes 5898244 | tf_op jit(solution)/shard_map/while
  466.0 25.9 %copy-start.7 = (bf16[2,768,640]{1,2,0:T(8,128)(2,1)S(1)}, bf16[2,768,640]{1,2,0:T(8,128)(2,1)}, u32[]{:S(2)}) copy-start(bf16[2,768,640]{1,2,0:T(8,128)(2,1)} %get-tuple-element.544) | copy-start | bytes 5898244 | tf_op jit(solution)/shard_map/while
  497.7 25.9 %copy-start.7 = (bf16[2,768,640]{1,2,0:T(8,128)(2,1)S(1)}, bf16[2,768,640]{1,2,0:T(8,128)(2,1)}, u32[]{:S(2)}) copy-start(bf16[2,768,640]{1,2,0:T(8,128)(2,1)} %get-tuple-element.544) | copy-start | bytes 5898244 | tf_op jit(solution)/shard_map/while
  529.3 25.9 %copy-start.7 = (bf16[2,768,640]{1,2,0:T(8,128)(2,1)S(1)}, bf16[2,768,640]{1,2,0:T(8,128)(2,1)}, u32[]{:S(2)}) copy-start(bf16[2,768,640]{1,2,0:T(8,128)(2,1)} %get-tuple-element.544) | copy-start | bytes 5898244 | tf_op jit(solution)/shard_map/while
  716.5 0.6 copy-start.8
  811.3 8.7 %copy-start.1 = (s32[2,768]{1,0:T(2,128)S(1)}, s32[2,768]{1,0:T(2,128)}, u32[]{:S(2)}) copy-start(s32[2,768]{1,0:T(2,128)} %param.11) | copy-start | bytes 18436
Sparse Core Ops, SparseCore 0:
  717.3 86.0 all-reduce.3
where the time goes:
time: 837 us; the launch traced here: 827 us
  other arithmetic  250 us (30%)
  matrix products  218 us (26%)
  waiting for transfers between devices  151 us (18%)
  local copies, waits for them, and re-layouts  102 us (12%)
  blocking collectives  67.2 us (8%)
  starting transfers between devices  18.4 us (2%)
  between operations  14.9 us (2%)
    another operation x13, other arithmetic  210 us
    psum x1, waiting for transfers between devices, local(): lax.psum((spectra, gram_matrix, trace_power), 'chan')  82 us
    psum x1, blocking collectives, local(): lax.psum((spectra, gram_matrix, trace_power), 'chan')  67.2 us
    all_to_all x1, waiting for transfers between devices, local(): lax.all_to_all(spectrum, 'chan', split_axis=1, concat_axis=2, tiled=True)  38 us
    dot_general x4, matrix products, project(): jnp.einsum('kml,rfl->krfm', members, dft_table, preferred_element_type=jn...  36.2 us
    dot_general x4, matrix products, temporal_advance(): jnp.einsum(layout, dft_table, segment, preferred_element_type=jnp.float32)  32.2 us
    all_to_all x1, waiting for transfers between devices, local(): lax.all_to_all(frequency_filter(local_spectrum, band_edges), 'chan', spli...  30.8 us
    dot_general x4, matrix products, rotate(): sin_imag = jnp.einsum(layout, sin_table, imag_part, precision=highest)  30.2 us
  transfers between devices with their start and end apart: 3, of which 3 were waited for; matrix products, arithmetic and copies ran while one was open for 2% of the time, Pallas kernels for 0%

commit v1 on v0

--- a/solution.py
+++ b/solution.py
@@ -158,13 +158,10 @@
     local_spectrum = lax.all_to_all(spectrum, "chan", split_axis=1, concat_axis=2, tiled=True)
     bin_count = local_spectrum.shape[1]
     band_edges = lax.dynamic_slice_in_dim(bounds, position * bin_count, bin_count, 1)
-    filtered = lax.all_to_all(
-        frequency_filter(local_spectrum, band_edges),
-        "chan",
-        split_axis=2,
-        concat_axis=1,
-        tiled=True,
-    )
+    here_x = frequency_filter(local_spectrum, band_edges)
+    carry = jnp.stack(jnp.split(here_x, jax.lax.axis_size("chan"), axis=2), 0)
+    even = jax.lax.all_to_all(carry, axis_name="chan", split_axis=0, concat_axis=0)
+    filtered = jnp.concatenate(even, 1)
     spectra = coefficient_spectra(basis, filtered, layout, frequencies, recorded_readings)
     flattened = basis.reshape(basis_rank, channels * tap_count)
     gram_matrix = jnp.einsum("ka,ja->kj", flattened, flattened, preferred_element_type=jnp.float32)

time: 837 us -> 800 us (0.956)
  local copies, waits for them, and re-layouts: 102 us -> 63.6 us
    all_to_all x2 -> x1, local copies, waits for them, and re-layouts: 18.4 us -> 1.71 us  [local(): jax.lax.all_to_all(carry, axis_name='chan', split_axis=0, concat_axis=0)]
    convert_element_type x3 -> x0, local copies, waits for them, and re-layouts: 15 us -> none  [the longest x1 11.3 us: frequency_filter(): return restored.astype(jnp.bfloat16)]
    unnamed x15 -> x26, local copies, waits for them, and re-layouts: 21.9 us -> 14.7 us
where the time goes in v1:
time: 800 us; the launch traced here: 791 us
  other arithmetic  252 us (32%)
  matrix products  218 us (27%)
  waiting for transfers between devices  151 us (19%)
  blocking collectives  67.2 us (8%)
  local copies, waits for them, and re-layouts  63.6 us (8%)
  starting transfers between devices  18.4 us (2%)
  between operations  14.9 us (2%)
    another operation x13, other arithmetic  211 us
    psum x1, waiting for transfers between devices, local(): lax.psum((spectra, gram_matrix, trace_power), 'chan')  82 us
    psum x1, blocking collectives, local(): lax.psum((spectra, gram_matrix, trace_power), 'chan')  67.2 us
    all_to_all x1, waiting for transfers between devices, local(): lax.all_to_all(spectrum, 'chan', split_axis=1, concat_axis=2, tiled=True)  38 us
    dot_general x4, matrix products, project(): jnp.einsum('kml,rfl->krfm', members, dft_table, preferred_element_type=jn...  36.2 us
    dot_general x4, matrix products, temporal_advance(): jnp.einsum(layout, dft_table, segment, preferred_element_type=jnp.float32)  32.2 us
    all_to_all x1, waiting for transfers between devices, local(): jax.lax.all_to_all(carry, axis_name='chan', split_axis=0, concat_axis=0)  30.6 us
    dot_general x4, matrix products, rotate(): sin_imag = jnp.einsum(layout, sin_table, imag_part, precision=highest)  30.2 us
  transfers between devices with their start and end apart: 3, of which 3 were waited for; matrix products, arithmetic and copies ran while one was open for 2% of the time, Pallas kernels for 0%

profile of v1, /device:TPU:0, one launch (start us, length us, event | category | flops | bytes accessed | tf_op | source)
XLA Modules:
  0.0 790.8 jit_solution(15219746097190486472)
XLA Ops:
  7.2 148.7 %while.40 = (s32[]{:T(128)}, f32[2,768,640]{2,1,0:T(8,128)}, s32[4]{0:T(128)S(1)}, bf16[640,7680]{1,0:T(8,128)(2,1)}, s32[]{:T(128)}, /*index=5*/s32[]{:T(128)}, s32[1]{0:T(128)}, s32[]{:T(128)}) while((s32[]{:T(128)}, f32[2,768,640]{2,1,0:T(8,128)}, s32[4]{0:T(128)S(1)}, bf16[640,7680]{1,0:T(8,128)(2,1)}, s32[]{:T(128)}, ...), condition=%wide.region_1.2_spmd.clone.clone, body=%wide.region_0.1_spmd.clone.clone.sunk | while | flops 3806337792 | bytes 53588192 | solution.py:60
  8.5 25.9 %fusion.349 = (bf16[1,768,1920]{2,1,0:T(8,128)(2,1)S(1)}, bf16[1,768,1920]{2,1,0:T(8,128)(2,1)S(1)}) fusion(f32[768]{0:T(1024)S(1)} %get-tuple-element.485, f32[768]{0:T(1024)S(1)} %get-tuple-element.486), kind=kLoop, calls=%fused_computation.52.clone.1 | loop fusion | flops 26542080 | bytes 5904384 | tf_op jit(solution)/shard_map/convert
  45.7 25.9 %fusion.349 = (bf16[1,768,1920]{2,1,0:T(8,128)(2,1)S(1)}, bf16[1,768,1920]{2,1,0:T(8,128)(2,1)S(1)}) fusion(f32[768]{0:T(1024)S(1)} %get-tuple-element.485, f32[768]{0:T(1024)S(1)} %get-tuple-element.486), kind=kLoop, calls=%fused_computation.52.clone.1 | loop fusion | flops 26542080 | bytes 5904384 | tf_op jit(solution)/shard_map/convert
  82.9 25.9 %fusion.349 = (bf16[1,768,1920]{2,1,0:T(8,128)(2,1)S(1)}, bf16[1,768,1920]{2,1,0:T(8,128)(2,1)S(1)}) fusion(f32[768]{0:T(1024)S(1)} %get-tuple-element.485, f32[768]{0:T(1024)S(1)} %get-tuple-element.486), kind=kLoop, calls=%fused_computation.52.clone.1 | loop fusion | flops 26542080 | bytes 5904384 | tf_op jit(solution)/shard_map/convert
  120.1 25.9 %fusion.349 = (bf16[1,768,1920]{2,1,0:T(8,128)(2,1)S(1)}, bf16[1,768,1920]{2,1,0:T(8,128)(2,1)S(1)}) fusion(f32[768]{0:T(1024)S(1)} %get-tuple-element.485, f32[768]{0:T(1024)S(1)} %get-tuple-element.486), kind=kLoop, calls=%fused_computation.52.clone.1 | loop fusion | flops 26542080 | bytes 5904384 | tf_op jit(solution)/shard_map/convert
  170.5 38.0 %all-to-all-done = bf16[2,768,640]{2,0,1:T(2,128)(2,1)S(1)} async-done(((bf16[2,768,640]{2,0,1:T(2,128)(2,1)}), bf16[2,768,640]{2,0,1:T(2,128)(2,1)S(1)}, u32[]{:S(2)}, u32[]{:S(2)}) %all-to-all-start) | async-done | bytes 1966112 | tf_op jit(solution)/shard_map/all_to_all | solution.py:158
  213.6 11.9 %fusion.89 = f32[48,16,640]{2,1,0:T(8,128)S(1)} fusion(f32[48,640,16]{1,2,0:T(8,128)S(1)} %multiply_add_fusion.1, f32[48,640,16]{1,2,0:T(8,128)S(1)} %multiply_subtract_fusion.1, f32[16,640]{1,0:T(8,128)S(1)} %get-tuple-element.371, f32[16,640]{1,0:T(8,128)S(1)} %get-tuple-element.370), kind=kOutput, calls=%fused_computation.124 | convolution fusion | flops 3780034560 | bytes 5980160 | tf_op jit(solution)/shard_map/mn,fkm->fkn/dot_general | solution.py:22
  225.5 11.7 %fusion.91 = f32[48,16,640]{2,1,0:T(8,128)S(1)} fusion(f32[48,640,16]{1,2,0:T(8,128)S(1)} %multiply_add_fusion.1, f32[48,640,16]{1,2,0:T(8,128)S(1)} %multiply_subtract_fusion.1, f32[16,640]{1,0:T(8,128)S(1)} %get-tuple-element.371, f32[16,640]{1,0:T(8,128)S(1)} %get-tuple-element.370), kind=kOutput, calls=%fused_computation.126 | convolution fusion | flops 3780034560 | bytes 5980160 | tf_op jit(solution)/shard_map/mn,fkm->fkn/dot_general | solution.py:23
  237.3 11.8 %add_select_fusion.6 = f32[48,16,640]{2,1,0:T(8,128)S(1)} fusion(f32[48,16,640]{2,1,0:T(8,128)S(1)} %fusion.89, s32[16,640]{1,0:T(8,128)S(1)} %compare_select_fusion, s32[48]{0:T(128)S(1)} %get-tuple-element.367, s32[48]{0:T(128)S(1)} %get-tuple-element.366, f32[48,640,16]{1,2,0:T(8,128)S(1)} %multiply_add_fusion.1, ...), kind=kOutput, calls=%fused_computation.113 | convolution fusion | flops 3782983680 | bytes 7987584 | tf_op jit(solution)/shard_map/mn,fkm->fkn/dot_general | solution.py:21
  249.0 11.8 %fusion.87 = f32[48,16,640]{2,1,0:T(8,128)S(1)} fusion(f32[48,16,640]{2,1,0:T(8,128)S(1)} %add_select_fusion.6), kind=kOutput, calls=%fused_computation.122 | convolution fusion | flops 3778560000 | bytes 3932160 | tf_op jit(solution)/shard_map/mn,fkn->fkm/dot_general | solution.py:23
  260.9 11.7 %subtract_select_fusion = f32[48,16,640]{2,1,0:T(8,128)S(1)} fusion(f32[48,16,640]{2,1,0:T(8,128)S(1)} %fusion.91, s32[16,640]{1,0:T(8,128)S(1)} %compare_select_fusion, s32[48]{0:T(128)S(1)} %get-tuple-element.367, s32[48]{0:T(128)S(1)} %get-tuple-element.366, f32[48,640,16]{1,2,0:T(8,128)S(1)} %multiply_add_fusion.1, ...), kind=kOutput, calls=%fused_computation.114 | convolution fusion | flops 3782983680 | bytes 7987584 | tf_op jit(solution)/shard_map/mn,fkm->fkn/dot_general | solution.py:20
  272.6 11.6 %fusion.85 = f32[48,16,640]{2,1,0:T(8,128)S(1)} fusion(f32[48,16,640]{2,1,0:T(8,128)S(1)} %subtract_select_fusion), kind=kOutput, calls=%fused_computation.120 | convolution fusion | flops 3778560000 | bytes 3932160 | tf_op jit(solution)/shard_map/mn,fkn->fkm/dot_general | solution.py:22
  284.2 11.9 %fusion.114 = f32[48,16,640]{2,1,0:T(8,128)S(1)} fusion(f32[48,16,640]{2,1,0:T(8,128)S(1)} %fusion.87, f32[48,16,640]{2,1,0:T(8,128)S(1)} %subtract_select_fusion), kind=kOutput, calls=%fused_computation.142 | convolution fusion | flops 3779051520 | bytes 5898240 | tf_op jit(solution)/shard_map/mn,fkn->fkm/dot_general | solution.py:20
  296.2 11.5 %fusion.117 = f32[48,16,640]{2,1,0:T(8,128)S(1)} fusion(f32[48,16,640]{2,1,0:T(8,128)S(1)} %fusion.85, f32[48,16,640]{2,1,0:T(8,128)S(1)} %add_select_fusion.6), kind=kOutput, calls=%fused_computation.143 | convolution fusion | flops 3779051520 | bytes 5898240 | tf_op jit(solution)/shard_map/mn,fkn->fkm/dot_general | solution.py:21
  340.3 10.7 %all-to-all-start.1 = ((bf16[16,2,48,640]{3,2,1,0:T(8,128)(2,1)}), bf16[16,2,48,640]{3,2,1,0:T(8,128)(2,1)}, u32[]{:S(2)}, u32[]{:S(2)}) async-start(bf16[16,2,48,640]{3,2,1,0:T(8,128)(2,1)} %fusion.190), calls=%async_computation.1 | async-start | bytes 3932160 | tf_op jit(solution)/shard_map/all_to_all | solution.py:163
  359.2 30.6 %all-to-all-done.1 = bf16[16,2,48,640]{3,2,1,0:T(8,128)(2,1)} async-done(((bf16[16,2,48,640]{3,2,1,0:T(8,128)(2,1)}), bf16[16,2,48,640]{3,2,1,0:T(8,128)(2,1)}, u32[]{:S(2)}, u32[]{:S(2)}) %all-to-all-start.1) | async-done | bytes 1966112 | tf_op jit(solution)/shard_map/all_to_all | solution.py:163
  397.3 126.7 %while.39 = (s32[]{:T(128)}, f32[4,1920]{1,0:T(4,128)S(1)}, s32[4]{0:T(128)S(1)}, bf16[2,768,640]{1,2,0:T(8,128)(2,1)}, s32[]{:T(128)}, /*index=5*/s32[1]{0:T(128)}, s32[]{:T(128)}) while((s32[]{:T(128)}, f32[4,1920]{1,0:T(4,128)S(1)}, s32[4]{0:T(128)S(1)}, bf16[2,768,640]{1,2,0:T(8,128)(2,1)}, s32[]{:T(128)}, ...), condition=%wide.region_11.12_spmd.clone.clone, body=%wide.region_9.11_spmd.clone.clone.sunk | while | flops 3808056064 | bytes 21677712 | solution.py:141
  398.6 25.9 %fusion.344 = (bf16[1,768,1920]{2,1,0:T(8,128)(2,1)S(1)}, bf16[1,768,1920]{2,1,0:T(8,128)(2,1)S(1)}) fusion(f32[768]{0:T(1024)S(1)} %get-tuple-element.477, f32[768]{0:T(1024)S(1)} %get-tuple-element.478), kind=kLoop, calls=%fused_computation.16.clone.1 | loop fusion | flops 26542080 | bytes 5904384 | tf_op jit(solution)/shard_map/convert.2
  430.3 25.9 %fusion.344 = (bf16[1,768,1920]{2,1,0:T(8,128)(2,1)S(1)}, bf16[1,768,1920]{2,1,0:T(8,128)(2,1)S(1)}) fusion(f32[768]{0:T(1024)S(1)} %get-tuple-element.477, f32[768]{0:T(1024)S(1)} %get-tuple-element.478), kind=kLoop, calls=%fused_computation.16.clone.1 | loop fusion | flops 26542080 | bytes 5904384 | tf_op jit(solution)/shard_map/convert.2
  462.0 25.9 %fusion.344 = (bf16[1,768,1920]{2,1,0:T(8,128)(2,1)S(1)}, bf16[1,768,1920]{2,1,0:T(8,128)(2,1)S(1)}) fusion(f32[768]{0:T(1024)S(1)} %get-tuple-element.477, f32[768]{0:T(1024)S(1)} %get-tuple-element.478), kind=kLoop, calls=%fused_computation.16.clone.1 | loop fusion | flops 26542080 | bytes 5904384 | tf_op jit(solution)/shard_map/convert.2
  493.6 25.9 %fusion.344 = (bf16[1,768,1920]{2,1,0:T(8,128)(2,1)S(1)}, bf16[1,768,1920]{2,1,0:T(8,128)(2,1)S(1)}) fusion(f32[768]{0:T(1024)S(1)} %get-tuple-element.477, f32[768]{0:T(1024)S(1)} %get-tuple-element.478), kind=kLoop, calls=%fused_computation.16.clone.1 | loop fusion | flops 26542080 | bytes 5904384 | tf_op jit(solution)/shard_map/convert.2
  524.0 67.2 %all-reduce.1 = (f32[16,16]{0,1:T(8,128)S(1)}, f32[7680]{0:T(1024)S(1)}) all-reduce(f32[16,16]{0,1:T(8,128)S(1)} %fusion.142, f32[7680]{0:T(1024)S(1)} %reshape.553), channel_id=1, replica_groups=mesh['groups'=2,'chan'=16] {'chan'}, use_global_device_ids=true, to_apply=%region_5.6 | all-reduce | flops 7936 | bytes 63488 | tf_op jit(solution)/shard_map/psum | solution.py:169
  595.1 84.8 %while.38 = (s32[]{:T(128)}, f32[4,4,2,768]{3,2,1,0:T(2,128)S(1)}, bf16[4,4,640,200]{2,3,1,0:T(8,128)(2,1)}, bf16[2,768,200]{1,2,0:T(8,128)(2,1)S(1)}, f32[768,640]{1,0:T(8,128)}, /*index=5*/f32[768,640]{1,0:T(8,128)}, s32[]{:T(128)}) while((s32[]{:T(128)}, f32[4,4,2,768]{3,2,1,0:T(2,128)S(1)}, bf16[4,4,640,200]{2,3,1,0:T(8,128)(2,1)}, ...), condition=%wide.region_3.4_spmd, body=%wide.region_2.3_spmd.sunk | while | flops 1588592640 | bytes 45113436 | solution.py:123
  684.7 82.0 %all-reduce.4.cloned.1.call-done = f32[16,2,768]{2,1,0:T(2,128)} async-done(((f32[16,2,768]{2,1,0:T(2,128)}), f32[16,2,768]{2,1,0:T(2,128)}) %all-reduce.4.cloned.1.call-update) | async-done | bytes 98320 | tf_op jit(solution)/shard_map/psum | solution.py:169
  (175 shorter events, 240.2 us)
Async XLA Ops:
  7.2 162.8 %copy-start = (s32[2,768]{1,0:T(2,128)S(1)}, s32[2,768]{1,0:T(2,128)}, u32[]{:S(2)}) copy-start(s32[2,768]{1,0:T(2,128)} %param.11) | copy-start | bytes 18436
  8.5 25.9 %copy-start.4 = (f32[2,768,640]{2,1,0:T(8,128)S(1)}, f32[2,768,640]{2,1,0:T(8,128)}, u32[]{:S(2)}) copy-start(f32[2,768,640]{2,1,0:T(8,128)} %get-tuple-element.498) | copy-start | bytes 11796484 | tf_op jit(solution)/shard_map/while
  42.5 1.9 copy-start.5
  45.7 25.9 %copy-start.4 = (f32[2,768,640]{2,1,0:T(8,128)S(1)}, f32[2,768,640]{2,1,0:T(8,128)}, u32[]{:S(2)}) copy-start(f32[2,768,640]{2,1,0:T(8,128)} %get-tuple-element.498) | copy-start | bytes 11796484 | tf_op jit(solution)/shard_map/while
  79.7 1.9 copy-start.5
  82.9 25.9 %copy-start.4 = (f32[2,768,640]{2,1,0:T(8,128)S(1)}, f32[2,768,640]{2,1,0:T(8,128)}, u32[]{:S(2)}) copy-start(f32[2,768,640]{2,1,0:T(8,128)} %get-tuple-element.498) | copy-start | bytes 11796484 | tf_op jit(solution)/shard_map/while
  116.9 1.9 copy-start.5
  120.1 25.9 %copy-start.4 = (f32[2,768,640]{2,1,0:T(8,128)S(1)}, f32[2,768,640]{2,1,0:T(8,128)}, u32[]{:S(2)}) copy-start(f32[2,768,640]{2,1,0:T(8,128)} %get-tuple-element.498) | copy-start | bytes 11796484 | tf_op jit(solution)/shard_map/while
  154.1 1.9 copy-start.5
  162.4 46.1 %all-to-all-start = ((bf16[2,768,640]{2,0,1:T(2,128)(2,1)}), bf16[2,768,640]{2,0,1:T(2,128)(2,1)S(1)}, u32[]{:S(2)}, u32[]{:S(2)}) async-start(bf16[2,768,640]{2,0,1:T(2,128)(2,1)} %copy.113), calls=%async_computation | async-start | bytes 3932160 | tf_op jit(solution)/shard_map/all_to_all | solution.py:158
  307.7 5.4 copy-start.2
  324.7 2.9 copy-start.3
  340.3 49.5 %all-to-all-start.1 = ((bf16[16,2,48,640]{3,2,1,0:T(8,128)(2,1)}), bf16[16,2,48,640]{3,2,1,0:T(8,128)(2,1)}, u32[]{:S(2)}, u32[]{:S(2)}) async-start(bf16[16,2,48,640]{3,2,1,0:T(8,128)(2,1)} %fusion.190), calls=%async_computation.1 | async-start | bytes 3932160 | tf_op jit(solution)/shard_map/all_to_all | solution.py:163
  351.0 415.7 %all-reduce.4.cloned.1.call-start = ((), (), s32[]{:S(2)}) async-start(), calls=%async_computation.2 | async-start | bytes 196608 | tf_op jit(solution)/shard_map/psum | solution.py:169
  398.6 25.9 %copy-start.6 = (bf16[2,768,640]{1,2,0:T(8,128)(2,1)S(1)}, bf16[2,768,640]{1,2,0:T(8,128)(2,1)}, u32[]{:S(2)}) copy-start(bf16[2,768,640]{1,2,0:T(8,128)(2,1)} %get-tuple-element.530) | copy-start | bytes 5898244 | tf_op jit(solution)/shard_map/while
  430.3 25.9 %copy-start.6 = (bf16[2,768,640]{1,2,0:T(8,128)(2,1)S(1)}, bf16[2,768,640]{1,2,0:T(8,128)(2,1)}, u32[]{:S(2)}) copy-start(bf16[2,768,640]{1,2,0:T(8,128)(2,1)} %get-tuple-element.530) | copy-start | bytes 5898244 | tf_op jit(solution)/shard_map/while
  462.0 25.9 %copy-start.6 = (bf16[2,768,640]{1,2,0:T(8,128)(2,1)S(1)}, bf16[2,768,640]{1,2,0:T(8,128)(2,1)}, u32[]{:S(2)}) copy-start(bf16[2,768,640]{1,2,0:T(8,128)(2,1)} %get-tuple-element.530) | copy-start | bytes 5898244 | tf_op jit(solution)/shard_map/while
  493.6 25.9 %copy-start.6 = (bf16[2,768,640]{1,2,0:T(8,128)(2,1)S(1)}, bf16[2,768,640]{1,2,0:T(8,128)(2,1)}, u32[]{:S(2)}) copy-start(bf16[2,768,640]{1,2,0:T(8,128)(2,1)} %get-tuple-element.530) | copy-start | bytes 5898244 | tf_op jit(solution)/shard_map/while
  679.9 0.6 copy-start.7
  774.7 8.7 %copy-start.1 = (s32[2,768]{1,0:T(2,128)S(1)}, s32[2,768]{1,0:T(2,128)}, u32[]{:S(2)}) copy-start(s32[2,768]{1,0:T(2,128)} %param.11) | copy-start | bytes 18436
Sparse Core Ops, SparseCore 0:
  680.6 86.0 all-reduce.3
